TPU v7x, 512 devices: a whole 4x8x8 slice. The times are simulated.
512 devices in a mesh: edp: 16 (over z, core), ep: 32 (over y, x).
Axes of the slice: x: 4, y: 8, z: 8, core: 2. Of those that a mesh axis runs over, the one named last changes fastest.
Arguments:
- token_acts: bfloat16 [16, 32, 2, 64, 1024], P('edp', 'ep'), may hold values from -6 to 6
- out_grad: bfloat16 [16, 32, 3584, 128], P('edp', 'ep'), may hold values from -0.59765625 to 0.59765625
- counts: int32 [16, 32, 2], P('edp', 'ep'), may hold values from 1 to 64, as said below
- params: float32 [32, 3584, 1024], P('ep', 'edp'), may hold values from -3 to 3
- first_moment: bfloat16 [32, 3584, 1024], P('ep', 'edp'), may hold values from -3 to 3
- second_moment: bfloat16 [32, 3584, 1024], P('ep', 'edp'), may hold values from 0.049804688 to 2
- old_expert: int32 [32], replicated, may hold values from 0 to 31, each once
- replica_of: int32 [32], replicated, may hold values from 0 to 31
- new_expert: int32 [32], replicated, may hold values from 0 to 31, each once
Outputs:
- update_step: float32 [32, 3584, 1024], P('ep', 'edp')
- new_first: bfloat16 [32, 3584, 1024], P('ep', 'edp')
- new_second: bfloat16 [32, 3584, 1024], P('ep', 'edp')
Inputs may be any that keep to these rules, and one draw needn't show every extreme that they name: `counts`: every slot has at least one live token; some slot is full and some slot has exactly one live token in every draw. `old_expert`: each expert appears exactly once. `new_expert`: each expert appears exactly once. `replica_of`: any expert may be served by any number of replica slots, its owner's included.
All inputs are finite; a program needn't handle non-finite values.
Results may differ from a plain program's by a relative error of at most 0.015.
Values may be sent and summed in bfloat16 or wider, within the bound.
A program may use at most 64 MiB of HBM per device.

v0:
```python
import jax
import jax.numpy as jnp
from jax import lax
from jax.sharding import PartitionSpec as P

beta_one = 0.9
beta_two = 0.95
bias_one = 0.9999734386011124
bias_two = 0.994079470779666
decay_rate = 0.1
adam_eps = 1e-08


def adam_update(weights, first_old, second_old, gradient):
    first_new = beta_one * first_old.astype(jnp.float32) + (1.0 - beta_one) * gradient
    second_new = beta_two * second_old.astype(jnp.float32) + (1.0 - beta_two) * gradient * gradient
    scaled = first_new / bias_one / (jnp.sqrt(second_new / bias_two) + adam_eps)
    step_new = -(scaled + decay_rate * weights)
    return (step_new, first_new.astype(jnp.bfloat16), second_new.astype(jnp.bfloat16))


def local(
    token_acts,
    out_grad,
    counts,
    params,
    first_moment,
    second_moment,
    old_expert,
    replica_of,
    new_expert,
):
    groups = lax.axis_size("edp")
    owners = lax.axis_size("ep")
    model_width = out_grad.shape[2]
    slot_count = token_acts.shape[2]
    tok_slot = token_acts.shape[3]
    hidden_units = token_acts.shape[4]
    row_count = model_width // groups
    piece_len = row_count * hidden_units // owners
    local_grad = out_grad[0, 0]
    local_counts = counts[0, 0]
    column = jnp.arange(slot_count * tok_slot, dtype=jnp.int32)
    slot_index = column // tok_slot
    live_limit = jnp.where(slot_index == 0, local_counts[0], local_counts[1])
    live_mask = column % tok_slot < live_limit
    masked = jnp.where(live_mask[None, :], local_grad, jnp.zeros_like(local_grad))
    received = lax.all_to_all(
        masked.reshape(groups, row_count, slot_count * tok_slot),
        "edp",
        split_axis=0,
        concat_axis=0,
        tiled=True,
    )
    arrived = lax.all_gather(token_acts[0], "edp", axis=0, tiled=True)
    count_here = arrived.shape[0]
    grad_block = received
    grad_block = grad_block.reshape(count_here, row_count, slot_count, tok_slot)
    slot_grads = jnp.einsum(
        "adst,astf->sdf", grad_block, arrived, preferred_element_type=jnp.float32
    )
    own_grad = slot_grads[0].reshape(owners, piece_len)
    replica_grad = slot_grads[1].reshape(owners, piece_len)
    sum_matrix = (replica_of[None, :] == old_expert[:, None]).astype(jnp.float32)
    move_matrix = (old_expert[None, :] == new_expert[:, None]).astype(jnp.float32)
    weights = params[0].reshape(owners, piece_len)
    first_old = first_moment[0].reshape(owners, piece_len)
    second_old = second_moment[0].reshape(owners, piece_len)
    replica_sent = lax.all_to_all(
        replica_grad.astype(jnp.bfloat16), "ep", split_axis=0, concat_axis=0, tiled=True
    ).astype(replica_grad.dtype)
    set_sums = jnp.dot(sum_matrix, replica_sent, precision=lax.Precision.HIGHEST)
    returned = lax.all_to_all(
        set_sums.astype(jnp.bfloat16), "ep", split_axis=0, concat_axis=0, tiled=True
    ).astype(set_sums.dtype)
    weights, first_old, second_old = adam_update(
        weights, first_old, second_old, own_grad + returned
    )
    weight_pieces = lax.all_to_all(weights, "ep", split_axis=0, concat_axis=0, tiled=True)
    first_pieces, second_pieces = (
        lax.all_to_all(first_old, "ep", split_axis=0, concat_axis=0, tiled=True),
        lax.all_to_all(second_old, "ep", split_axis=0, concat_axis=0, tiled=True),
    )
    placed_steps = jnp.dot(move_matrix, weight_pieces, precision=lax.Precision.HIGHEST)
    move_half = move_matrix.astype(jnp.bfloat16)
    placed_first = jnp.dot(move_half, first_pieces, preferred_element_type=jnp.float32).astype(
        jnp.bfloat16
    )
    placed_second = jnp.dot(move_half, second_pieces, preferred_element_type=jnp.float32).astype(
        jnp.bfloat16
    )
    final_steps = lax.all_to_all(placed_steps, "ep", split_axis=0, concat_axis=0, tiled=True)
    final_first, final_second = (
        lax.all_to_all(placed_first, "ep", split_axis=0, concat_axis=0, tiled=True),
        lax.all_to_all(placed_second, "ep", split_axis=0, concat_axis=0, tiled=True),
    )
    return (
        final_steps.reshape(1, row_count, hidden_units),
        final_first.reshape(1, row_count, hidden_units),
        final_second.reshape(1, row_count, hidden_units),
    )


def solution(mesh):
    return jax.shard_map(
        local,
        mesh=mesh,
        in_specs=(
            P("edp", "ep", None, None, None),
            P("edp", "ep", None, None),
            P("edp", "ep", None),
            P("ep", "edp", None),
            P("ep", "edp", None),
            P("ep", "edp", None),
            P(),
            P(),
            P(),
        ),
        out_specs=(P("ep", "edp", None), P("ep", "edp", None), P("ep", "edp", None)),
        check_vma=False,
    )
```

profile of v0, /device:TPU:2, one launch (start us, length us, event | category | flops | bytes accessed | tf_op | source)
XLA Modules:
  0.0 280.3 jit_solution(12393630941862970195)
XLA Ops:
  11.8 41.0 %all_to_all.77 = bf16[16,224,128]{2,1,0:T(8,128)(2,1)S(1)} all-to-all(bf16[16,224,128]{2,1,0:T(8,128)(2,1)S(1)} %broadcast_select_fusion), channel_id=1, replica_groups=mesh['edp'=16,'ep'=32] {'edp'}, dimensions={0} | all-to-all | bytes 1835008 | tf_op jit(solution)/shard_map/all_to_all | solution.py:48
  53.3 18.0 %all-gather.3.cloned.1.call-done = bf16[16,1,2,64,1024]{4,3,2,1,0:T(8,128)(2,1)} async-done(((bf16[1,1,2,64,1024]{4,3,2,1,0:T(8,128)(2,1)}), bf16[16,1,2,64,1024]{4,3,2,1,0:T(8,128)(2,1)}) %all-gather.3.cloned.1.call-update) | async-done | bytes 4194320 | tf_op jit(solution)/shard_map/all_gather | solution.py:55
  71.3 3.3 %fusion.5 = f32[2,224,1024]{2,1,0:T(8,128)S(1)} fusion(bf16[16,224,2,64]{1,3,2,0:T(8,128)(2,1)S(1)} %bitcast.32, bf16[16,1,2,64,1024]{4,3,2,1,0:T(8,128)(2,1)} %all-gather.3.cloned.1.call-done), kind=kOutput, calls=%fused_computation.9 | convolution fusion | flops 939524096 | bytes 6946816 | tf_op jit(solution)/shard_map/adst,astf->sdf/dot_general | solution.py:59
  75.7 3.3 %reduce.3 = bf16[32,7168]{1,0:T(8,128)(2,1)S(1)} reduce(bf16[32,1,7168]{2,1,0:T(2,128)(2,1)S(1)} %convert_element_type.77, bf16[]{:T(256)} %broadcast.125), dimensions={1}, to_apply=%convert_element_type.77.reduce_sub_computation | reduce | bytes 917506 | tf_op jit(solution)/shard_map/convert_element_type | solution.py:70
  79.3 25.9 %all_to_all.78 = bf16[32,2,3584]{2,1,0:T(2,128)(2,1)S(1)} all-to-all(bf16[32,2,3584]{2,1,0:T(2,128)(2,1)S(1)} %reshape.144), channel_id=1, replica_groups=mesh['edp'=16,'ep'=32] {'ep'}, dimensions={0} | all-to-all | bytes 917504 | tf_op jit(solution)/shard_map/all_to_all | solution.py:69
  107.8 5.6 %all-to-all-start.2 = ((bf16[32,2,3584]{2,1,0:T(2,128)(2,1)}), bf16[32,2,3584]{2,1,0:T(2,128)(2,1)S(1)}, u32[]{:S(2)}, u32[]{:S(2)}) async-start(bf16[32,2,3584]{2,1,0:T(2,128)(2,1)} %reshape.146), calls=%async_computation.2 | async-start | bytes 917504 | tf_op jit(solution)/shard_map/all_to_all | solution.py:73
  113.4 2.2 broadcast_multiply_fusion
  119.3 2.6 mul.67
  123.9 2.5 mul.71
  130.2 3.1 %fusion.32 = (bf16[32,1,7168]{2,0,1:T(8,128)(2,1)}, f32[32,1,7168]{2,0,1:T(8,128)S(1)}, bf16[32,1,7168]{2,0,1:T(8,128)(2,1)S(1)}) fusion(f32[32,1,7168]{2,0,1:T(8,128)} %mul.71, f32[32,1,7168]{2,0,1:T(8,128)S(1)} %reshape_squeeze.2, bf16[32,1,7168]{2,1,0:T(2,128)(2,1)} %reshape.147, f32[32,1,7168]{2,0,1:T(8,128)S(1)} %mul.76, f32[32,1,7168]{2,0,1:T(8,128)} %mul.67), kind=kLoop, calls=%fused_computation.47 | loop fusion | flops 3440640 | bytes 5963776 | tf_op jit(solution)/shard_map/convert_element_type | solution.py:19
  136.3 9.8 %all-to-all-start.7 = ((bf16[32,2,3584]{2,1,0:T(2,128)(2,1)}), bf16[32,2,3584]{2,1,0:T(2,128)(2,1)S(1)}, u32[]{:S(2)}, u32[]{:S(2)}) async-start(bf16[32,2,3584]{2,1,0:T(2,128)(2,1)} %reshape.152), calls=%async_computation.7 | async-start | bytes 917504 | tf_op jit(solution)/shard_map/all_to_all | solution.py:82
  148.0 12.1 %all-to-all-done.7 = bf16[32,2,3584]{2,1,0:T(2,128)(2,1)S(1)} async-done(((bf16[32,2,3584]{2,1,0:T(2,128)(2,1)}), bf16[32,2,3584]{2,1,0:T(2,128)(2,1)S(1)}, u32[]{:S(2)}, u32[]{:S(2)}) %all-to-all-start.7) | async-done | bytes 458784 | tf_op jit(solution)/shard_map/all_to_all | solution.py:82
  160.1 5.7 %all-to-all-start.5 = ((bf16[32,2,3584]{2,1,0:T(2,128)(2,1)}), bf16[32,2,3584]{2,1,0:T(2,128)(2,1)S(1)}, u32[]{:S(2)}, u32[]{:S(2)}) async-start(bf16[32,2,3584]{2,1,0:T(2,128)(2,1)} %reshape.148), calls=%async_computation.5 | async-start | bytes 917504 | tf_op jit(solution)/shard_map/all_to_all | solution.py:81
  168.6 10.7 %all-to-all-done.5 = bf16[32,2,3584]{2,1,0:T(2,128)(2,1)S(1)} async-done(((bf16[32,2,3584]{2,1,0:T(2,128)(2,1)}), bf16[32,2,3584]{2,1,0:T(2,128)(2,1)S(1)}, u32[]{:S(2)}, u32[]{:S(2)}) %all-to-all-start.5) | async-done | bytes 458784 | tf_op jit(solution)/shard_map/all_to_all | solution.py:81
  179.3 5.6 %all-to-all-start.8 = ((bf16[32,2,3584]{2,1,0:T(2,128)(2,1)}), bf16[32,2,3584]{2,1,0:T(2,128)(2,1)S(1)}, u32[]{:S(2)}, u32[]{:S(2)}) async-start(bf16[32,2,3584]{2,1,0:T(2,128)(2,1)} %reshape.154), calls=%async_computation.8 | async-start | bytes 917504 | tf_op jit(solution)/shard_map/all_to_all | solution.py:95
  186.7 11.1 %all-to-all-done.8 = bf16[32,2,3584]{2,1,0:T(2,128)(2,1)S(1)} async-done(((bf16[32,2,3584]{2,1,0:T(2,128)(2,1)}), bf16[32,2,3584]{2,1,0:T(2,128)(2,1)S(1)}, u32[]{:S(2)}, u32[]{:S(2)}) %all-to-all-start.8) | async-done | bytes 458784 | tf_op jit(solution)/shard_map/all_to_all | solution.py:95
  197.9 5.6 %all-to-all-start.3 = ((f32[32,1,7168]{2,1,0:T(1,128)}), f32[32,1,7168]{2,1,0:T(1,128)S(1)}, u32[]{:S(2)}, u32[]{:S(2)}) async-start(f32[32,1,7168]{2,1,0:T(1,128)} %copy.35), calls=%async_computation.3 | async-start | bytes 1835008 | tf_op jit(solution)/shard_map/all_to_all | solution.py:79
  206.1 19.8 %all-to-all-done.3 = f32[32,1,7168]{2,1,0:T(1,128)S(1)} async-done(((f32[32,1,7168]{2,1,0:T(1,128)}), f32[32,1,7168]{2,1,0:T(1,128)S(1)}, u32[]{:S(2)}, u32[]{:S(2)}) %all-to-all-start.3) | async-done | bytes 917536 | tf_op jit(solution)/shard_map/all_to_all | solution.py:79
  225.9 5.6 %all-to-all-start.6 = ((bf16[32,2,3584]{2,1,0:T(2,128)(2,1)}), bf16[32,2,3584]{2,1,0:T(2,128)(2,1)S(1)}, u32[]{:S(2)}, u32[]{:S(2)}) async-start(bf16[32,2,3584]{2,1,0:T(2,128)(2,1)} %reshape.150), calls=%async_computation.6 | async-start | bytes 917504 | tf_op jit(solution)/shard_map/all_to_all | solution.py:94
  234.0 9.8 %all-to-all-done.6 = bf16[32,2,3584]{2,1,0:T(2,128)(2,1)S(1)} async-done(((bf16[32,2,3584]{2,1,0:T(2,128)(2,1)}), bf16[32,2,3584]{2,1,0:T(2,128)(2,1)S(1)}, u32[]{:S(2)}, u32[]{:S(2)}) %all-to-all-start.6) | async-done | bytes 458784 | tf_op jit(solution)/shard_map/all_to_all | solution.py:94
  243.7 5.6 %all-to-all-start.4 = ((f32[32,1,7168]{2,1,0:T(1,128)}), f32[32,1,7168]{2,1,0:T(1,128)S(1)}, u32[]{:S(2)}, u32[]{:S(2)}) async-start(f32[32,1,7168]{2,1,0:T(1,128)} %copy.36), calls=%async_computation.4 | async-start | bytes 1835008 | tf_op jit(solution)/shard_map/all_to_all | solution.py:92
  249.7 2.7 reduce.2
  254.1 2.7 reduce.1
  258.1 12.1 %all-to-all-done.4 = f32[32,1,7168]{2,1,0:T(1,128)S(1)} async-done(((f32[32,1,7168]{2,1,0:T(1,128)}), f32[32,1,7168]{2,1,0:T(1,128)S(1)}, u32[]{:S(2)}, u32[]{:S(2)}) %all-to-all-start.4) | async-done | bytes 917536 | tf_op jit(solution)/shard_map/all_to_all | solution.py:92
  (48 shorter events, 39.6 us)
Async XLA Ops:
  7.2 64.1 %all-gather.3.cloned.1.call-start = ((), (), s32[]{:S(2)}) async-start(), calls=%async_computation.9 | async-start | bytes 4456448 | tf_op jit(solution)/shard_map/all_gather | solution.py:55
  74.7 30.9 %copy-start = (s32[32]{0:T(128)S(1)}, s32[32]{0:T(128)}, u32[]{:S(2)}) copy-start(s32[32]{0:T(128)} %param.15) | copy-start | bytes 388
  74.7 30.9 %copy-start.2 = (s32[32]{0:T(128)S(1)}, s32[32]{0:T(128)}, u32[]{:S(2)}) copy-start(s32[32]{0:T(128)} %param.16) | copy-start | bytes 388
  107.8 21.2 %all-to-all-start.2 = ((bf16[32,2,3584]{2,1,0:T(2,128)(2,1)}), bf16[32,2,3584]{2,1,0:T(2,128)(2,1)S(1)}, u32[]{:S(2)}, u32[]{:S(2)}) async-start(bf16[32,2,3584]{2,1,0:T(2,128)(2,1)} %reshape.146), calls=%async_computation.2 | async-start | bytes 917504 | tf_op jit(solution)/shard_map/all_to_all | solution.py:73
  133.3 33.0 %copy-start.1 = (s32[32]{0:T(128)S(1)}, s32[32]{0:T(128)}, u32[]{:S(2)}) copy-start(s32[32]{0:T(128)} %param.17) | copy-start | bytes 388
  136.3 23.9 %all-to-all-start.7 = ((bf16[32,2,3584]{2,1,0:T(2,128)(2,1)}), bf16[32,2,3584]{2,1,0:T(2,128)(2,1)S(1)}, u32[]{:S(2)}, u32[]{:S(2)}) async-start(bf16[32,2,3584]{2,1,0:T(2,128)(2,1)} %reshape.152), calls=%async_computation.7 | async-start | bytes 917504 | tf_op jit(solution)/shard_map/all_to_all | solution.py:82
  160.1 19.2 %all-to-all-start.5 = ((bf16[32,2,3584]{2,1,0:T(2,128)(2,1)}), bf16[32,2,3584]{2,1,0:T(2,128)(2,1)S(1)}, u32[]{:S(2)}, u32[]{:S(2)}) async-start(bf16[32,2,3584]{2,1,0:T(2,128)(2,1)} %reshape.148), calls=%async_computation.5 | async-start | bytes 917504 | tf_op jit(solution)/shard_map/all_to_all | solution.py:81
  179.3 18.6 %all-to-all-start.8 = ((bf16[32,2,3584]{2,1,0:T(2,128)(2,1)}), bf16[32,2,3584]{2,1,0:T(2,128)(2,1)S(1)}, u32[]{:S(2)}, u32[]{:S(2)}) async-start(bf16[32,2,3584]{2,1,0:T(2,128)(2,1)} %reshape.154), calls=%async_computation.8 | async-start | bytes 917504 | tf_op jit(solution)/shard_map/all_to_all | solution.py:95
  197.9 28.0 %all-to-all-start.3 = ((f32[32,1,7168]{2,1,0:T(1,128)}), f32[32,1,7168]{2,1,0:T(1,128)S(1)}, u32[]{:S(2)}, u32[]{:S(2)}) async-start(f32[32,1,7168]{2,1,0:T(1,128)} %copy.35), calls=%async_computation.3 | async-start | bytes 1835008 | tf_op jit(solution)/shard_map/all_to_all | solution.py:79
  225.9 17.8 %all-to-all-start.6 = ((bf16[32,2,3584]{2,1,0:T(2,128)(2,1)}), bf16[32,2,3584]{2,1,0:T(2,128)(2,1)S(1)}, u32[]{:S(2)}, u32[]{:S(2)}) async-start(bf16[32,2,3584]{2,1,0:T(2,128)(2,1)} %reshape.150), calls=%async_computation.6 | async-start | bytes 917504 | tf_op jit(solution)/shard_map/all_to_all | solution.py:94
  243.7 26.5 %all-to-all-start.4 = ((f32[32,1,7168]{2,1,0:T(1,128)}), f32[32,1,7168]{2,1,0:T(1,128)S(1)}, u32[]{:S(2)}, u32[]{:S(2)}) async-start(f32[32,1,7168]{2,1,0:T(1,128)} %copy.36), calls=%async_computation.4 | async-start | bytes 1835008 | tf_op jit(solution)/shard_map/all_to_all | solution.py:92
Sparse Core Ops, SparseCore 0:
  10.1 61.1 all-gather.2
where the time goes:
time: 282 us; the launch traced here: 280 us
  waiting for transfers between devices  94.3 us (33%)
  blocking collectives  66.9 us (24%)
  starting transfers between devices  43.4 us (15%)
  local copies, waits for them, and re-layouts  28.2 us (10%)
  other arithmetic  28.2 us (10%)
  between operations  14.3 us (5%)
  matrix products  4.97 us (2%)
    all_to_all x1, blocking collectives, local(): lax.all_to_all(masked.reshape(groups, row_count, slot_count * tok_slot),...  41 us
    all_to_all x1, blocking collectives, local(): lax.all_to_all(replica_grad.astype(jnp.bfloat16), 'ep', split_axis=0, con...  25.9 us
    all_to_all x1, waiting for transfers between devices, local(): lax.all_to_all(weights, 'ep', split_axis=0, concat_axis=0, tiled=True)  19.8 us
    all_gather x1, waiting for transfers between devices, local(): arrived = lax.all_gather(token_acts[0], 'edp', axis=0, tiled=True)  18 us
    all_to_all x1, waiting for transfers between devices, local(): lax.all_to_all(second_old, 'ep', split_axis=0, concat_axis=0, tiled=True)  12.1 us
    all_to_all x1, waiting for transfers between devices, local(): lax.all_to_all(placed_steps, 'ep', split_axis=0, concat_axis=0, tiled=True)  12.1 us
    all_to_all x1, waiting for transfers between devices, local(): lax.all_to_all(placed_second, 'ep', split_axis=0, concat_axis=0, tiled=True)  11.1 us
    all_to_all x1, waiting for transfers between devices, local(): lax.all_to_all(first_old, 'ep', split_axis=0, concat_axis=0, tiled=True)  10.7 us
  transfers between devices with their start and end apart: 8, of which 7 were waited for; matrix products, arithmetic and copies ran while one was open for 14% of the time, Pallas kernels for 0%

commit v1 on v0

--- a/solution.py
+++ b/solution.py
@@ -9,6 +9,28 @@
 bias_two = 0.994079470779666
 decay_rate = 0.1
 adam_eps = 1e-08
+
+
+def laid_out(blocks, dim):
+    blocks = jnp.moveaxis(blocks, 0, dim)
+    shape = blocks.shape
+    return blocks.reshape(*shape[:dim], shape[dim] * shape[dim + 1], *shape[dim + 2 :])
+
+
+def ring_gather(x, axis, dim):
+    count = lax.axis_size(axis)
+    pairs = [(i, (i + 1) % count) for i in range(count)]
+    back = [(b, a) for a, b in pairs]
+    lower, upper = ([], [])
+    for turn in range(count - 1):
+        if turn % 2 == 0:
+            lower.append(lax.ppermute(lower[-1] if lower else x, axis, pairs))
+        else:
+            upper.append(lax.ppermute(upper[-1] if upper else x, axis, back))
+    blocks = jnp.stack([*lower[::-1], x, *upper])
+    shift = lax.axis_index(axis) - len(lower)
+    blocks = blocks[(jnp.arange(count) - shift) % count]
+    return laid_out(blocks, dim)
 
 
 def adam_update(weights, first_old, second_old, gradient):
@@ -52,7 +74,7 @@
         concat_axis=0,
         tiled=True,
     )
-    arrived = lax.all_gather(token_acts[0], "edp", axis=0, tiled=True)
+    arrived = ring_gather(token_acts[0], "edp", 0)
     count_here = arrived.shape[0]
     grad_block = received
     grad_block = grad_block.reshape(count_here, row_count, slot_count, tok_slot)

time: 282 us -> 313 us (1.11)
  the two profiles are of different devices: /device:TPU:2 before, /device:TPU:192 now
where the time goes in v1:
time: 313 us; the launch traced here: 311 us
  waiting for transfers between devices  126 us (40%)
  starting transfers between devices  73.6 us (24%)
  local copies, waits for them, and re-layouts  53.4 us (17%)
  other arithmetic  29 us (9%)
  blocking collectives  23.2 us (7%)
  matrix products  4.97 us (2%)
    ppermute x7, waiting for transfers between devices, ring_gather(): upper.append(lax.ppermute(upper[-1] if upper else x, axis, back))  31.4 us
    unnamed x51, local copies, waits for them, and re-layouts  27.4 us
    all_to_all x1, blocking collectives, local(): lax.all_to_all(replica_grad.astype(jnp.bfloat16), 'ep', split_axis=0, con...  23.2 us
    all_to_all x1, waiting for transfers between devices, local(): lax.all_to_all(weights, 'ep', split_axis=0, concat_axis=0, tiled=True)  21.8 us
    ppermute x8, starting transfers between devices, ring_gather(): lower.append(lax.ppermute(lower[-1] if lower else x, axis, pairs))  15.6 us
    all_to_all x1, waiting for transfers between devices, local(): lax.all_to_all(placed_first, 'ep', split_axis=0, concat_axis=0, tiled=True)  15.1 us
    all_to_all x1, waiting for transfers between devices, local(): lax.all_to_all(placed_steps, 'ep', split_axis=0, concat_axis=0, tiled=True)  15 us
    all_to_all x1, waiting for transfers between devices, local(): lax.all_to_all(second_old, 'ep', split_axis=0, concat_axis=0, tiled=True)  14.1 us
  transfers between devices with their start and end apart: 23, of which 13 were waited for; matrix products, arithmetic and copies ran while one was open for 19% of the time, Pallas kernels for 0%

profile of v1, /device:TPU:192, one launch (start us, length us, event | category | flops | bytes accessed | tf_op | source)
XLA Modules:
  0.0 311.5 jit_solution(5077016182521271707)
XLA Ops:
  3.3 3.4 %collective-permute-done = bf16[1,2,64,1024]{3,2,1,0:T(8,128)(2,1)S(1)} collective-permute-done((bf16[1,2,64,1024]{3,2,1,0:T(8,128)(2,1)}, bf16[1,2,64,1024]{3,2,1,0:T(8,128)(2,1)S(1)}, u32[]{:S(2)}, u32[]{:S(2)}) %collective-permute-start) | collective-permute-done | bytes 262176 | tf_op jit(solution)/shard_map/ppermute | solution.py:27
  10.1 8.4 %all-to-all-start = ((bf16[16,224,128]{2,1,0:T(8,128)(2,1)}), bf16[16,224,128]{2,1,0:T(8,128)(2,1)S(1)}, u32[]{:S(2)}, u32[]{:S(2)}) async-start(bf16[16,224,128]{2,1,0:T(8,128)(2,1)} %broadcast_select_fusion), calls=%async_computation | async-start | bytes 1835008 | tf_op jit(solution)/shard_map/all_to_all | solution.py:70
  19.1 23.0 %collective-permute-done.8 = bf16[1,2,64,1024]{3,2,1,0:T(8,128)(2,1)S(1)} collective-permute-done((bf16[1,2,64,1024]{3,2,1,0:T(8,128)(2,1)}, bf16[1,2,64,1024]{3,2,1,0:T(8,128)(2,1)S(1)}, u32[]{:S(2)}, u32[]{:S(2)}) %collective-permute-start.8) | collective-permute-done | bytes 262176 | tf_op jit(solution)/shard_map/ppermute | solution.py:29
  44.8 3.0 collective-permute-done.9
  62.1 3.7 %collective-permute-start.6 = (bf16[1,2,64,1024]{3,2,1,0:T(8,128)(2,1)S(1)}, bf16[1,2,64,1024]{3,2,1,0:T(8,128)(2,1)}, u32[]{:S(2)}, u32[]{:S(2)}) collective-permute-start(bf16[1,2,64,1024]{3,2,1,0:T(8,128)(2,1)S(1)} %collective-permute-done.5), channel_id=1, source_target_pairs={{0,32},{32,64},{64,96},{96,128},{128,160},{160,192},{192,224},{224... | collective-permute-start | bytes 786440 | tf_op jit(solution)/shard_map/ppermute | solution.py:27
  68.2 4.7 %collective-permute-start.7 = (bf16[1,2,64,1024]{3,2,1,0:T(8,128)(2,1)}, bf16[1,2,64,1024]{3,2,1,0:T(8,128)(2,1)}, u32[]{:S(2)}, u32[]{:S(2)}) collective-permute-start(bf16[1,2,64,1024]{3,2,1,0:T(8,128)(2,1)} %collective-permute-done.6), channel_id=1, source_target_pairs={{0,32},{32,64},{64,96},{96,128},{128,160},{160,192},{192,224},{224... | collective-permute-start | bytes 786440 | tf_op jit(solution)/shard_map/ppermute | solution.py:27
  95.1 5.0 %gather_fusion = bf16[16,2,64,1024]{3,2,1,0:T(8,128)(2,1)} fusion(bf16[16,2,64,1024]{3,2,1,0:T(8,128)(2,1)} %bitcast.20, s32[1024]{0:T(1024)S(1)} %pad_clamp_fusion), kind=kCustom, calls=%fused_computation | custom fusion | bytes 8388672 | tf_op jit(solution)/shard_map/gather | solution.py:32
  100.1 3.3 %convolution_bitcast_fusion.1 = f32[2,224,1024]{2,1,0:T(8,128)S(1)} fusion(bf16[16,224,2,64]{1,3,2,0:T(8,128)(2,1)S(1)} %bitcast.62, bf16[16,2,64,1024]{3,2,1,0:T(8,128)(2,1)} %gather_fusion), kind=kOutput, calls=%fused_computation.8 | convolution fusion | flops 939524096 | bytes 6946816 | tf_op jit(solution)/shard_map/adst,astf->sdf/dot_general | solution.py:81
  104.4 3.3 %reduce.3 = bf16[32,7168]{1,0:T(8,128)(2,1)S(1)} reduce(bf16[32,1,7168]{2,1,0:T(2,128)(2,1)S(1)} %convert_element_type.77, bf16[]{:T(256)} %broadcast.194), dimensions={1}, to_apply=%convert_element_type.77.reduce_sub_computation | reduce | bytes 917506 | tf_op jit(solution)/shard_map/convert_element_type | solution.py:92
  108.0 23.2 %all_to_all.77 = bf16[32,2,3584]{2,1,0:T(2,128)(2,1)S(1)} all-to-all(bf16[32,2,3584]{2,1,0:T(2,128)(2,1)S(1)} %reshape.207), channel_id=1, replica_groups=mesh['edp'=16,'ep'=32] {'ep'}, dimensions={0} | all-to-all | bytes 917504 | tf_op jit(solution)/shard_map/all_to_all | solution.py:91
  133.8 4.3 %all-to-all-start.2 = ((bf16[32,2,3584]{2,1,0:T(2,128)(2,1)}), bf16[32,2,3584]{2,1,0:T(2,128)(2,1)S(1)}, u32[]{:S(2)}, u32[]{:S(2)}) async-start(bf16[32,2,3584]{2,1,0:T(2,128)(2,1)} %reshape.209), calls=%async_computation.2 | async-start | bytes 917504 | tf_op jit(solution)/shard_map/all_to_all | solution.py:95
  154.9 3.1 %fusion.29 = (bf16[32,1,7168]{2,0,1:T(8,128)(2,1)S(1)}, f32[32,1,7168]{2,0,1:T(8,128)S(1)}, bf16[32,1,7168]{2,0,1:T(8,128)(2,1)}) fusion(f32[32,1,7168]{2,0,1:T(8,128)} %mul.71, f32[32,1,7168]{2,0,1:T(8,128)S(1)} %reshape_squeeze.2, bf16[32,1,7168]{2,1,0:T(2,128)(2,1)} %reshape.210, f32[32,1,7168]{2,0,1:T(8,128)} %mul.76, f32[32,1,7168]{2,0,1:T(8,128)S(1)} %mul.67), kind=kLoop, calls=%fused_computation.69 | loop fusion | flops 3440640 | bytes 5963776 | tf_op jit(solution)/shard_map/convert_element_type | solution.py:41
  161.0 9.6 %all-to-all-start.5 = ((bf16[32,2,3584]{2,1,0:T(2,128)(2,1)}), bf16[32,2,3584]{2,1,0:T(2,128)(2,1)S(1)}, u32[]{:S(2)}, u32[]{:S(2)}) async-start(bf16[32,2,3584]{2,1,0:T(2,128)(2,1)} %reshape.211), calls=%async_computation.5 | async-start | bytes 917504 | tf_op jit(solution)/shard_map/all_to_all | solution.py:103
  172.6 12.4 %all-to-all-done.5 = bf16[32,2,3584]{2,1,0:T(2,128)(2,1)S(1)} async-done(((bf16[32,2,3584]{2,1,0:T(2,128)(2,1)}), bf16[32,2,3584]{2,1,0:T(2,128)(2,1)S(1)}, u32[]{:S(2)}, u32[]{:S(2)}) %all-to-all-start.5) | async-done | bytes 458784 | tf_op jit(solution)/shard_map/all_to_all | solution.py:103
  184.9 6.1 %all-to-all-start.7 = ((bf16[32,2,3584]{2,1,0:T(2,128)(2,1)}), bf16[32,2,3584]{2,1,0:T(2,128)(2,1)S(1)}, u32[]{:S(2)}, u32[]{:S(2)}) async-start(bf16[32,2,3584]{2,1,0:T(2,128)(2,1)} %reshape.215), calls=%async_computation.7 | async-start | bytes 917504 | tf_op jit(solution)/shard_map/all_to_all | solution.py:104
  193.7 14.1 %all-to-all-done.7 = bf16[32,2,3584]{2,1,0:T(2,128)(2,1)S(1)} async-done(((bf16[32,2,3584]{2,1,0:T(2,128)(2,1)}), bf16[32,2,3584]{2,1,0:T(2,128)(2,1)S(1)}, u32[]{:S(2)}, u32[]{:S(2)}) %all-to-all-start.7) | async-done | bytes 458784 | tf_op jit(solution)/shard_map/all_to_all | solution.py:104
  207.8 5.2 %all-to-all-start.6 = ((bf16[32,2,3584]{2,1,0:T(2,128)(2,1)}), bf16[32,2,3584]{2,1,0:T(2,128)(2,1)S(1)}, u32[]{:S(2)}, u32[]{:S(2)}) async-start(bf16[32,2,3584]{2,1,0:T(2,128)(2,1)} %reshape.213), calls=%async_computation.6 | async-start | bytes 917504 | tf_op jit(solution)/shard_map/all_to_all | solution.py:116
  214.9 15.1 %all-to-all-done.6 = bf16[32,2,3584]{2,1,0:T(2,128)(2,1)S(1)} async-done(((bf16[32,2,3584]{2,1,0:T(2,128)(2,1)}), bf16[32,2,3584]{2,1,0:T(2,128)(2,1)S(1)}, u32[]{:S(2)}, u32[]{:S(2)}) %all-to-all-start.6) | async-done | bytes 458784 | tf_op jit(solution)/shard_map/all_to_all | solution.py:116
  230.0 4.4 %all-to-all-start.3 = ((f32[32,1,7168]{2,1,0:T(1,128)}), f32[32,1,7168]{2,1,0:T(1,128)S(1)}, u32[]{:S(2)}, u32[]{:S(2)}) async-start(f32[32,1,7168]{2,1,0:T(1,128)} %copy.34), calls=%async_computation.3 | async-start | bytes 1835008 | tf_op jit(solution)/shard_map/all_to_all | solution.py:101
  237.1 21.8 %all-to-all-done.3 = f32[32,1,7168]{2,1,0:T(1,128)S(1)} async-done(((f32[32,1,7168]{2,1,0:T(1,128)}), f32[32,1,7168]{2,1,0:T(1,128)S(1)}, u32[]{:S(2)}, u32[]{:S(2)}) %all-to-all-start.3) | async-done | bytes 917536 | tf_op jit(solution)/shard_map/all_to_all | solution.py:101
  258.9 5.5 %all-to-all-start.8 = ((bf16[32,2,3584]{2,1,0:T(2,128)(2,1)}), bf16[32,2,3584]{2,1,0:T(2,128)(2,1)S(1)}, u32[]{:S(2)}, u32[]{:S(2)}) async-start(bf16[32,2,3584]{2,1,0:T(2,128)(2,1)} %reshape.217), calls=%async_computation.8 | async-start | bytes 917504 | tf_op jit(solution)/shard_map/all_to_all | solution.py:117
  267.0 13.0 %all-to-all-done.8 = bf16[32,2,3584]{2,1,0:T(2,128)(2,1)S(1)} async-done(((bf16[32,2,3584]{2,1,0:T(2,128)(2,1)}), bf16[32,2,3584]{2,1,0:T(2,128)(2,1)S(1)}, u32[]{:S(2)}, u32[]{:S(2)}) %all-to-all-start.8) | async-done | bytes 458784 | tf_op jit(solution)/shard_map/all_to_all | solution.py:117
  280.0 4.4 %all-to-all-start.4 = ((f32[32,1,7168]{2,1,0:T(1,128)}), f32[32,1,7168]{2,1,0:T(1,128)S(1)}, u32[]{:S(2)}, u32[]{:S(2)}) async-start(f32[32,1,7168]{2,1,0:T(1,128)} %copy.35), calls=%async_computation.4 | async-start | bytes 1835008 | tf_op jit(solution)/shard_map/all_to_all | solution.py:114
  293.2 15.0 %all-to-all-done.4 = f32[32,1,7168]{2,1,0:T(1,128)S(1)} async-done(((f32[32,1,7168]{2,1,0:T(1,128)}), f32[32,1,7168]{2,1,0:T(1,128)S(1)}, u32[]{:S(2)}, u32[]{:S(2)}) %all-to-all-start.4) | async-done | bytes 917536 | tf_op jit(solution)/shard_map/all_to_all | solution.py:114
  (113 shorter events, 95.3 us)
Async XLA Ops:
  0.6 6.0 %collective-permute-start = (bf16[1,2,64,1024]{3,2,1,0:T(8,128)(2,1)}, bf16[1,2,64,1024]{3,2,1,0:T(8,128)(2,1)S(1)}, u32[]{:S(2)}, u32[]{:S(2)}) collective-permute-start(bf16[1,2,64,1024]{3,2,1,0:T(8,128)(2,1)} %bitcast.64), channel_id=1, source_target_pairs={{0,32},{32,64},{64,96},{96,128},{128,160},{160,192},{192,224},{224... | collective-permute-start | bytes 786440 | tf_op jit(solution)/shard_map/ppermute | solution.py:27
  6.7 12.2 %collective-permute-start.1 = (bf16[1,2,64,1024]{3,2,1,0:T(8,128)(2,1)S(1)}, bf16[1,2,64,1024]{3,2,1,0:T(8,128)(2,1)S(1)}, u32[]{:S(2)}, u32[]{:S(2)}) collective-permute-start(bf16[1,2,64,1024]{3,2,1,0:T(8,128)(2,1)S(1)} %collective-permute-done), channel_id=1, source_target_pairs={{0,32},{32,64},{64,96},{96,128},{128,160},{160,192},{192,224},{224... | collective-permute-start | bytes 786440 | tf_op jit(solution)/shard_map/ppermute | solution.py:27
  10.1 76.3 %copy-start = (bf16[1,1,2,64,1024]{4,3,2,1,0:T(8,128)(2,1)S(1)}, bf16[1,1,2,64,1024]{4,3,2,1,0:T(8,128)(2,1)}, u32[]{:S(2)}) copy-start(bf16[1,1,2,64,1024]{4,3,2,1,0:T(8,128)(2,1)} %param.9) | copy-start | bytes 786436
  10.1 64.2 %all-to-all-start = ((bf16[16,224,128]{2,1,0:T(8,128)(2,1)}), bf16[16,224,128]{2,1,0:T(8,128)(2,1)S(1)}, u32[]{:S(2)}, u32[]{:S(2)}) async-start(bf16[16,224,128]{2,1,0:T(8,128)(2,1)} %broadcast_select_fusion), calls=%async_computation | async-start | bytes 1835008 | tf_op jit(solution)/shard_map/all_to_all | solution.py:70
  18.6 23.5 %collective-permute-start.8 = (bf16[1,2,64,1024]{3,2,1,0:T(8,128)(2,1)}, bf16[1,2,64,1024]{3,2,1,0:T(8,128)(2,1)S(1)}, u32[]{:S(2)}, u32[]{:S(2)}) collective-permute-start(bf16[1,2,64,1024]{3,2,1,0:T(8,128)(2,1)} %bitcast.65), channel_id=1, source_target_pairs={{32,0},{64,32},{96,64},{128,96},{160,128},{192,160},{224,192},{256... | collective-permute-start | bytes 786440 | tf_op jit(solution)/shard_map/ppermute | solution.py:29
  18.9 25.0 %collective-permute-start.2 = (bf16[1,2,64,1024]{3,2,1,0:T(8,128)(2,1)S(1)}, bf16[1,2,64,1024]{3,2,1,0:T(8,128)(2,1)S(1)}, u32[]{:S(2)}, u32[]{:S(2)}) collective-permute-start(bf16[1,2,64,1024]{3,2,1,0:T(8,128)(2,1)S(1)} %collective-permute-done.1), channel_id=1, source_target_pairs={{0,32},{32,64},{64,96},{96,128},{128,160},{160,192},{192,224},{224... | collective-permute-start | bytes 786440 | tf_op jit(solution)/shard_map/ppermute | solution.py:27
  42.0 5.7 %collective-permute-start.9 = (bf16[1,2,64,1024]{3,2,1,0:T(8,128)(2,1)S(1)}, bf16[1,2,64,1024]{3,2,1,0:T(8,128)(2,1)S(1)}, u32[]{:S(2)}, u32[]{:S(2)}) collective-permute-start(bf16[1,2,64,1024]{3,2,1,0:T(8,128)(2,1)S(1)} %collective-permute-done.8), channel_id=1, source_target_pairs={{32,0},{64,32},{96,64},{128,96},{160,128},{192,160},{224,192},{256... | collective-permute-start | bytes 786440 | tf_op jit(solution)/shard_map/ppermute | solution.py:29
  43.9 6.0 %collective-permute-start.3 = (bf16[1,2,64,1024]{3,2,1,0:T(8,128)(2,1)S(1)}, bf16[1,2,64,1024]{3,2,1,0:T(8,128)(2,1)S(1)}, u32[]{:S(2)}, u32[]{:S(2)}) collective-permute-start(bf16[1,2,64,1024]{3,2,1,0:T(8,128)(2,1)S(1)} %collective-permute-done.2), channel_id=1, source_target_pairs={{0,32},{32,64},{64,96},{96,128},{128,160},{160,192},{192,224},{224... | collective-permute-start | bytes 786440 | tf_op jit(solution)/shard_map/ppermute | solution.py:27
  47.7 6.0 %collective-permute-start.10 = (bf16[1,2,64,1024]{3,2,1,0:T(8,128)(2,1)S(1)}, bf16[1,2,64,1024]{3,2,1,0:T(8,128)(2,1)S(1)}, u32[]{:S(2)}, u32[]{:S(2)}) collective-permute-start(bf16[1,2,64,1024]{3,2,1,0:T(8,128)(2,1)S(1)} %collective-permute-done.9), channel_id=1, source_target_pairs={{32,0},{64,32},{96,64},{128,96},{160,128},{192,160},{224,192},{256... | collective-permute-start | bytes 786440 | tf_op jit(solution)/shard_map/ppermute | solution.py:29
  49.9 6.1 %collective-permute-start.4 = (bf16[1,2,64,1024]{3,2,1,0:T(8,128)(2,1)S(1)}, bf16[1,2,64,1024]{3,2,1,0:T(8,128)(2,1)S(1)}, u32[]{:S(2)}, u32[]{:S(2)}) collective-permute-start(bf16[1,2,64,1024]{3,2,1,0:T(8,128)(2,1)S(1)} %collective-permute-done.3), channel_id=1, source_target_pairs={{0,32},{32,64},{64,96},{96,128},{128,160},{160,192},{192,224},{224... | collective-permute-start | bytes 786440 | tf_op jit(solution)/shard_map/ppermute | solution.py:27
  53.8 6.1 %collective-permute-start.11 = (bf16[1,2,64,1024]{3,2,1,0:T(8,128)(2,1)S(1)}, bf16[1,2,64,1024]{3,2,1,0:T(8,128)(2,1)S(1)}, u32[]{:S(2)}, u32[]{:S(2)}) collective-permute-start(bf16[1,2,64,1024]{3,2,1,0:T(8,128)(2,1)S(1)} %collective-permute-done.10), channel_id=1, source_target_pairs={{32,0},{64,32},{96,64},{128,96},{160,128},{192,160},{224,192},{256... | collective-permute-start | bytes 786440 | tf_op jit(solution)/shard_map/ppermute | solution.py:29
  56.0 6.1 %collective-permute-start.5 = (bf16[1,2,64,1024]{3,2,1,0:T(8,128)(2,1)S(1)}, bf16[1,2,64,1024]{3,2,1,0:T(8,128)(2,1)S(1)}, u32[]{:S(2)}, u32[]{:S(2)}) collective-permute-start(bf16[1,2,64,1024]{3,2,1,0:T(8,128)(2,1)S(1)} %collective-permute-done.4), channel_id=1, source_target_pairs={{0,32},{32,64},{64,96},{96,128},{128,160},{160,192},{192,224},{224... | collective-permute-start | bytes 786440 | tf_op jit(solution)/shard_map/ppermute | solution.py:27
  59.9 7.1 %collective-permute-start.12 = (bf16[1,2,64,1024]{3,2,1,0:T(8,128)(2,1)S(1)}, bf16[1,2,64,1024]{3,2,1,0:T(8,128)(2,1)}, u32[]{:S(2)}, u32[]{:S(2)}) collective-permute-start(bf16[1,2,64,1024]{3,2,1,0:T(8,128)(2,1)S(1)} %collective-permute-done.11), channel_id=1, source_target_pairs={{32,0},{64,32},{96,64},{128,96},{160,128},{192,160},{224,192},{256... | collective-permute-start | bytes 786440 | tf_op jit(solution)/shard_map/ppermute | solution.py:29
  62.1 6.1 %collective-permute-start.6 = (bf16[1,2,64,1024]{3,2,1,0:T(8,128)(2,1)S(1)}, bf16[1,2,64,1024]{3,2,1,0:T(8,128)(2,1)}, u32[]{:S(2)}, u32[]{:S(2)}) collective-permute-start(bf16[1,2,64,1024]{3,2,1,0:T(8,128)(2,1)S(1)} %collective-permute-done.5), channel_id=1, source_target_pairs={{0,32},{32,64},{64,96},{96,128},{128,160},{160,192},{192,224},{224... | collective-permute-start | bytes 786440 | tf_op jit(solution)/shard_map/ppermute | solution.py:27
  66.9 7.3 %collective-permute-start.13 = (bf16[1,2,64,1024]{3,2,1,0:T(8,128)(2,1)}, bf16[1,2,64,1024]{3,2,1,0:T(8,128)(2,1)}, u32[]{:S(2)}, u32[]{:S(2)}) collective-permute-start(bf16[1,2,64,1024]{3,2,1,0:T(8,128)(2,1)} %collective-permute-done.12), channel_id=1, source_target_pairs={{32,0},{64,32},{96,64},{128,96},{160,128},{192,160},{224,192},{256... | collective-permute-start | bytes 786440 | tf_op jit(solution)/shard_map/ppermute | solution.py:29
  68.2 6.7 %collective-permute-start.7 = (bf16[1,2,64,1024]{3,2,1,0:T(8,128)(2,1)}, bf16[1,2,64,1024]{3,2,1,0:T(8,128)(2,1)}, u32[]{:S(2)}, u32[]{:S(2)}) collective-permute-start(bf16[1,2,64,1024]{3,2,1,0:T(8,128)(2,1)} %collective-permute-done.6), channel_id=1, source_target_pairs={{0,32},{32,64},{64,96},{96,128},{128,160},{160,192},{192,224},{224... | collective-permute-start | bytes 786440 | tf_op jit(solution)/shard_map/ppermute | solution.py:27
  74.3 19.2 %collective-permute-start.14 = (bf16[1,2,64,1024]{3,2,1,0:T(8,128)(2,1)}, bf16[1,2,64,1024]{3,2,1,0:T(8,128)(2,1)}, u32[]{:S(2)}, u32[]{:S(2)}) collective-permute-start(bf16[1,2,64,1024]{3,2,1,0:T(8,128)(2,1)} %collective-permute-done.13), channel_id=1, source_target_pairs={{32,0},{64,32},{96,64},{128,96},{160,128},{192,160},{224,192},{256... | collective-permute-start | bytes 786440 | tf_op jit(solution)/shard_map/ppermute | solution.py:29
  133.8 19.9 %all-to-all-start.2 = ((bf16[32,2,3584]{2,1,0:T(2,128)(2,1)}), bf16[32,2,3584]{2,1,0:T(2,128)(2,1)S(1)}, u32[]{:S(2)}, u32[]{:S(2)}) async-start(bf16[32,2,3584]{2,1,0:T(2,128)(2,1)} %reshape.209), calls=%async_computation.2 | async-start | bytes 917504 | tf_op jit(solution)/shard_map/all_to_all | solution.py:95
  161.0 23.9 %all-to-all-start.5 = ((bf16[32,2,3584]{2,1,0:T(2,128)(2,1)}), bf16[32,2,3584]{2,1,0:T(2,128)(2,1)S(1)}, u32[]{:S(2)}, u32[]{:S(2)}) async-start(bf16[32,2,3584]{2,1,0:T(2,128)(2,1)} %reshape.211), calls=%async_computation.5 | async-start | bytes 917504 | tf_op jit(solution)/shard_map/all_to_all | solution.py:103
  184.9 22.9 %all-to-all-start.7 = ((bf16[32,2,3584]{2,1,0:T(2,128)(2,1)}), bf16[32,2,3584]{2,1,0:T(2,128)(2,1)S(1)}, u32[]{:S(2)}, u32[]{:S(2)}) async-start(bf16[32,2,3584]{2,1,0:T(2,128)(2,1)} %reshape.215), calls=%async_computation.7 | async-start | bytes 917504 | tf_op jit(solution)/shard_map/all_to_all | solution.py:104
  207.8 22.2 %all-to-all-start.6 = ((bf16[32,2,3584]{2,1,0:T(2,128)(2,1)}), bf16[32,2,3584]{2,1,0:T(2,128)(2,1)S(1)}, u32[]{:S(2)}, u32[]{:S(2)}) async-start(bf16[32,2,3584]{2,1,0:T(2,128)(2,1)} %reshape.213), calls=%async_computation.6 | async-start | bytes 917504 | tf_op jit(solution)/shard_map/all_to_all | solution.py:116
  230.0 28.9 %all-to-all-start.3 = ((f32[32,1,7168]{2,1,0:T(1,128)}), f32[32,1,7168]{2,1,0:T(1,128)S(1)}, u32[]{:S(2)}, u32[]{:S(2)}) async-start(f32[32,1,7168]{2,1,0:T(1,128)} %copy.34), calls=%async_computation.3 | async-start | bytes 1835008 | tf_op jit(solution)/shard_map/all_to_all | solution.py:101
  258.9 21.1 %all-to-all-start.8 = ((bf16[32,2,3584]{2,1,0:T(2,128)(2,1)}), bf16[32,2,3584]{2,1,0:T(2,128)(2,1)S(1)}, u32[]{:S(2)}, u32[]{:S(2)}) async-start(bf16[32,2,3584]{2,1,0:T(2,128)(2,1)} %reshape.217), calls=%async_computation.8 | async-start | bytes 917504 | tf_op jit(solution)/shard_map/all_to_all | solution.py:117
  280.0 28.2 %all-to-all-start.4 = ((f32[32,1,7168]{2,1,0:T(1,128)}), f32[32,1,7168]{2,1,0:T(1,128)S(1)}, u32[]{:S(2)}, u32[]{:S(2)}) async-start(f32[32,1,7168]{2,1,0:T(1,128)} %copy.35), calls=%async_computation.4 | async-start | bytes 1835008 | tf_op jit(solution)/shard_map/all_to_all | solution.py:114
  (11 other events, 224.9 us)
